TPU v7x, 32 devices: a whole 2x2x4 slice. The times are simulated.
32 devices in a mesh: band: 4 (over z), head: 4 (over y, x), dp: 2 (over core).
Axes of the slice: x: 2, y: 2, z: 4, core: 2. Of those that a mesh axis runs over, the one named last changes fastest.
Arguments:
- tokens: bfloat16 [32, 1024, 512], P(('dp', 'band'), None, 'head'), parts along dimension 0, may hold values from -6 to 6
- corner_row: int32 [2048], P('dp'), parts along dimension 0, may hold values from 0 to 14
- corner_col: int32 [2048], P('dp'), parts along dimension 0, may hold values from 0 to 1022
- fraction: float32 [2, 2048], P(None, 'dp'), parts along dimension 1, may hold values from 0 to 1
- w_query: bfloat16 [512, 512], P(None, 'head'), may hold values from -2 to 2
- w_key: bfloat16 [512, 512], P(None, 'head'), may hold values from -2 to 2
- w_value: bfloat16 [512, 512], P(None, 'head'), may hold values from -0.25 to 0.25
- w_out: bfloat16 [512, 512], P('head'), may hold values from -0.25 to 0.25
- conv_kernel: float32 [25, 512], P(None, 'head'), may hold values from -1.25 to 1.25
- norm_gain: float32 [512], replicated, may hold values from 0.1 to 1.9
Outputs:
- mixed: bfloat16 [32, 1024, 512], P(('dp', 'band'), None, 'head'), parts along dimension 0
There are 2 independent parts, one for each index of `dp`. A program takes and returns all parts, laid end to end along the dimension named above; an argument that names none is the same for every part. Nothing has to cross between parts.
All inputs are finite; a program needn't handle non-finite values.
Results may differ from a plain program's by a relative error of at most 0.029.
Values may be sent and summed in bfloat16 or wider, within the bound.
A program may use at most 64 MiB of HBM per device.

v0:
```python
import jax
import jax.numpy as jnp
from jax import lax
from jax.sharding import PartitionSpec as P

HEADS = 16
KER = 5


def padded_2(block, sides, width):
    for axis, dim in sides:
        count = lax.axis_size(axis)
        forward = [(i, i + 1) for i in range(count - 1)]
        backward = [(target, source) for source, target in forward]
        low = lax.ppermute(
            lax.slice_in_dim(block, block.shape[dim] - width, None, axis=dim), axis, forward
        )
        high = lax.ppermute(lax.slice_in_dim(block, 0, width, axis=dim), axis, backward)
        block = jnp.concatenate([low, block, high], axis=dim)
    return block


def layer_norm(values, norm_gain):
    values = values.astype(jnp.float32)
    center = jnp.mean(values, axis=-1, keepdims=True)
    spread = jnp.mean(jnp.square(values - center), axis=-1, keepdims=True)
    return ((values - center) * lax.rsqrt(spread + 1e-05) * norm_gain).astype(jnp.bfloat16)


def sample_points(normed, col_table, row_table, count):

    def add_row(index, total):
        plane = lax.dynamic_index_in_dim(normed, index, 0, keepdims=False)
        inner = jnp.dot(col_table, plane, preferred_element_type=jnp.float32)
        weight = lax.dynamic_index_in_dim(row_table, index, 1, keepdims=True)
        return total + weight * inner

    empty = jnp.zeros((count, normed.shape[2]), jnp.float32)
    return lax.fori_loop(0, normed.shape[0], add_row, empty)


def attend(query, key, value, heads):
    count, width = query.shape
    size = width // heads
    block = min(512, count)
    blocks = query.reshape(count // block, block, heads, size)
    key_heads = key.reshape(-1, heads, size)
    value_heads = value.reshape(-1, heads, size)
    scale = 1.0 / size**0.5

    def one_block(part):
        scores = (
            jnp.einsum("qhd,khd->hqk", part, key_heads, preferred_element_type=jnp.float32) * scale
        )
        top = jnp.max(scores, axis=-1, keepdims=True)
        expo = jnp.exp(scores - top)
        probs = (expo / jnp.sum(expo, axis=-1, keepdims=True)).astype(jnp.bfloat16)
        out = jnp.einsum("hqk,khd->qhd", probs, value_heads, preferred_element_type=jnp.float32)
        return out.astype(jnp.bfloat16).reshape(block, width)

    return lax.map(one_block, blocks).reshape(count, width)


def shards(
    tokens, corner_row, corner_col, fraction, w_query, w_key, w_value, w_out, conv_kernel, norm_gain
):
    band_rows, columns, channels = tokens.shape
    whole = lax.all_gather(tokens, "head", axis=2, tiled=True)
    normed = layer_norm(whole, norm_gain)
    width = normed.shape[2]
    count = band_rows * columns
    query = jnp.dot(
        normed.reshape(count, width), w_query, preferred_element_type=jnp.float32
    ).astype(jnp.bfloat16)
    channel_start = lax.axis_index("head") * channels
    normed_here = lax.dynamic_slice_in_dim(normed, channel_start, channels, 2)
    row_top = (1.0 - fraction[0]).astype(jnp.bfloat16)
    row_bottom = fraction[0].astype(jnp.bfloat16)
    col_left = (1.0 - fraction[1]).astype(jnp.bfloat16)
    col_right = fraction[1].astype(jnp.bfloat16)
    positions = lax.broadcasted_iota(jnp.int32, (1, columns), 1)
    zero_bf = jnp.zeros((), jnp.bfloat16)
    col_table = jnp.where(positions == corner_col[:, None], col_left[:, None], zero_bf) + jnp.where(
        positions == corner_col[:, None] + 1, col_right[:, None], zero_bf
    )
    band_start = lax.axis_index("band") * band_rows
    grid_rows = band_start + lax.broadcasted_iota(jnp.int32, (1, band_rows), 1)
    zero_f = jnp.zeros((), jnp.float32)
    row_table = jnp.where(
        grid_rows == corner_row[:, None], row_top.astype(jnp.float32)[:, None], zero_f
    ) + jnp.where(
        grid_rows == corner_row[:, None] + 1, row_bottom.astype(jnp.float32)[:, None], zero_f
    )
    points = corner_row.shape[0]
    share_rows = points // lax.axis_size("band")
    piece = lax.psum_scatter(
        sample_points(normed_here, col_table, row_table, share_rows * lax.axis_size("band")).astype(
            jnp.bfloat16
        ),
        "band",
        scatter_dimension=0,
        tiled=True,
    )
    share = lax.all_gather(piece, "head", axis=1, tiled=True)
    key_share = jnp.dot(share, w_key, preferred_element_type=jnp.float32).astype(jnp.bfloat16)
    value_share = jnp.dot(share, w_value, preferred_element_type=jnp.float32).astype(jnp.bfloat16)
    key, value = (
        lax.all_gather(key_share, "band", axis=0, tiled=True),
        lax.all_gather(value_share, "band", axis=0, tiled=True),
    )
    heads_here = HEADS // lax.axis_size("head")
    attended = attend(query, key, value, heads_here)
    partial_out = jnp.dot(attended, w_out, preferred_element_type=jnp.float32).reshape(
        band_rows, columns, width
    )
    projected = lax.psum_scatter(
        partial_out.astype(jnp.bfloat16), "head", scatter_dimension=2, tiled=True
    ).astype(jnp.float32)
    margin = KER // 2
    rimmed = padded_2(normed_here, (("band", 0),), margin)
    padded = jnp.pad(rimmed, ((0, 0), (margin, margin), (0, 0))).astype(jnp.float32)
    local = jnp.zeros((band_rows, columns, channels), jnp.float32)
    for first in range(KER):
        for second in range(KER):
            local = (
                local
                + conv_kernel[first * KER + second]
                * padded[first : first + band_rows, second : second + columns]
            )
    total = tokens.astype(jnp.float32) + projected + local
    return total.astype(jnp.bfloat16)


def solution(mesh):
    return jax.shard_map(
        shards,
        mesh=mesh,
        in_specs=(
            P(("dp", "band"), None, "head"),
            P("dp"),
            P("dp"),
            P(None, "dp"),
            P(None, "head"),
            P(None, "head"),
            P(None, "head"),
            P("head", None),
            P(None, "head"),
            P(),
        ),
        out_specs=P(("dp", "band"), None, "head"),
        check_vma=False,
    )
```

profile of v0, /device:TPU:0, one launch (start us, length us, event | category | flops | bytes accessed | tf_op | source)
XLA Modules:
  0.0 302.1 jit_solution(5138590391112813641)
XLA Ops:
  11.0 53.4 %all-gather.2.cloned.1.call-done = bf16[4,1024,512]{2,1,0:T(8,128)(2,1)} async-done(((bf16[4,1024,128]{2,1,0:T(8,128)(2,1)}), bf16[4,1024,512]{2,1,0:T(8,128)(2,1)}) %all-gather.2.cloned.1.call-update) | async-done | bytes 4194320 | tf_op jit(solution)/shard_map/all_gather | solution.py:68
  64.4 3.0 convert_reduce_fusion
  73.7 6.7 %while.25 = (s32[]{:T(128)}, f32[1024,128]{0,1:T(8,128)S(1)}, f32[1024,4]{0,1:T(4,128)S(1)}, bf16[4,1024,128]{2,1,0:T(8,128)(2,1)S(1)}, s32[1024]{0:T(1024)S(1)}...) while((s32[]{:T(128)}, f32[1024,128]{0,1:T(8,128)S(1)}, ...), condition=%wide.region_3.4_spmd.clone, body=%wide.region_2.3_spmd.clone.sunk | while | flops 277217280 | bytes 1335423 | solution.py:39
  81.2 3.4 %convolution_convert_fusion = bf16[4096,128]{1,0:T(8,128)(2,1)S(1)} fusion(bf16[4096,512]{1,0:T(8,128)(2,1)} %bitcast.130, bf16[512,128]{1,0:T(8,128)(2,1)S(1)} %copy-done.4), kind=kOutput, calls=%fused_computation.50 | convolution fusion | flops 537395200 | bytes 5373952 | tf_op jit(solution)/shard_map/dot_general | solution.py:72
  85.9 15.3 %reduce-scatter.5.cloned.1.call-done = bf16[256,128]{0,1:T(8,128)(2,1)} async-done(((bf16[1024,128]{0,1:T(8,128)(2,1)}), bf16[256,128]{0,1:T(8,128)(2,1)}) %reduce-scatter.5.cloned.1.call-update) | async-done | bytes 65552 | tf_op jit(solution)/shard_map/reduce_scatter | solution.py:96
  101.3 9.2 %all_gather.13 = bf16[256,512]{0,1:T(8,128)(2,1)S(1)} all-gather(bf16[256,128]{0,1:T(8,128)(2,1)} %reduce-scatter.5.cloned.1.call-done), channel_id=1, replica_groups=mesh['band'=4,'head'=4,'dp'=2] {'head'}, dimensions={1}, use_global_device_ids=true | all-gather | bytes 327680 | tf_op jit(solution)/shard_map/all_gather | solution.py:104
  111.0 14.3 %all_gather.14 = bf16[1024,128]{1,0:T(8,128)(2,1)S(1)} all-gather(bf16[256,128]{1,0:T(8,128)(2,1)S(1)} %convolution_convert_fusion.3), channel_id=1, replica_groups=mesh['band'=4,'head'=4,'dp'=2] {'band'}, dimensions={0}, use_global_device_ids=true | all-gather | bytes 327680 | tf_op jit(solution)/shard_map/all_gather | solution.py:108
  125.5 14.0 %all_gather.15 = bf16[1024,128]{1,0:T(8,128)(2,1)S(1)} all-gather(bf16[256,128]{1,0:T(8,128)(2,1)S(1)} %convolution_convert_fusion.2), channel_id=1, replica_groups=mesh['band'=4,'head'=4,'dp'=2] {'band'}, dimensions={0}, use_global_device_ids=true | all-gather | bytes 327680 | tf_op jit(solution)/shard_map/all_gather | solution.py:109
  139.7 54.7 %while.24 = (s32[]{:T(128)}, bf16[8,512,128]{2,1,0:T(8,128)(2,1)}, bf16[8,512,4,32]{1,3,2,0:T(8,128)(2,1)S(1)}, bf16[1024,4,32]{0,2,1:T(8,128)(2,1)S(1)}, bf16[1024,4,32]{0,2,1:T(8,128)(2,1)S(1)}, /*index=5*/s32[]{:T(128)}) while((s32[]{:T(128)}, bf16[8,512,128]{2,1,0:T(8,128)(2,1)}, bf16[8,512,4,32]{1,3,2,0:T(8,128)(2,1)S(1)}, ...), condition=%wide.region_8.9_spmd, body=%wide.region_5.8_spmd.sunk | while | flops 417402880 | bytes 1720409 | solution.py:61
  142.6 3.1 %fusion.148 = bf16[4,512,32]{1,2,0:T(8,128)(2,1)S(1)} fusion(bf16[1024,4,32]{0,2,1:T(8,128)(2,1)S(1)} %get-tuple-element.358, f32[4,512]{1,0:T(4,128)S(1)} %fusion.147, bf16[1024,4,32]{0,2,1:T(8,128)(2,1)S(1)} %get-tuple-element.357, bf16[8,512,4,32]{1,3,2,0:T(8,128)(2,1)S(1)} %get-tuple-element.356, s32[]{:T(128)S(6)} %copy.42), kind=kOutput, calls=%fused_computation.8.clone.1 | convolution fusion | flops 276892672 | bytes 794628 | tf_op jit(solution)/shard_map/while/body/eval_jaxpr/hqk,khd->qhd/dot_general | solution.py:58
  149.5 3.1 %fusion.148 = bf16[4,512,32]{1,2,0:T(8,128)(2,1)S(1)} fusion(bf16[1024,4,32]{0,2,1:T(8,128)(2,1)S(1)} %get-tuple-element.358, f32[4,512]{1,0:T(4,128)S(1)} %fusion.147, bf16[1024,4,32]{0,2,1:T(8,128)(2,1)S(1)} %get-tuple-element.357, bf16[8,512,4,32]{1,3,2,0:T(8,128)(2,1)S(1)} %get-tuple-element.356, s32[]{:T(128)S(6)} %copy.42), kind=kOutput, calls=%fused_computation.8.clone.1 | convolution fusion | flops 276892672 | bytes 794628 | tf_op jit(solution)/shard_map/while/body/eval_jaxpr/hqk,khd->qhd/dot_general | solution.py:58
  156.3 3.1 %fusion.148 = bf16[4,512,32]{1,2,0:T(8,128)(2,1)S(1)} fusion(bf16[1024,4,32]{0,2,1:T(8,128)(2,1)S(1)} %get-tuple-element.358, f32[4,512]{1,0:T(4,128)S(1)} %fusion.147, bf16[1024,4,32]{0,2,1:T(8,128)(2,1)S(1)} %get-tuple-element.357, bf16[8,512,4,32]{1,3,2,0:T(8,128)(2,1)S(1)} %get-tuple-element.356, s32[]{:T(128)S(6)} %copy.42), kind=kOutput, calls=%fused_computation.8.clone.1 | convolution fusion | flops 276892672 | bytes 794628 | tf_op jit(solution)/shard_map/while/body/eval_jaxpr/hqk,khd->qhd/dot_general | solution.py:58
  163.1 3.1 %fusion.148 = bf16[4,512,32]{1,2,0:T(8,128)(2,1)S(1)} fusion(bf16[1024,4,32]{0,2,1:T(8,128)(2,1)S(1)} %get-tuple-element.358, f32[4,512]{1,0:T(4,128)S(1)} %fusion.147, bf16[1024,4,32]{0,2,1:T(8,128)(2,1)S(1)} %get-tuple-element.357, bf16[8,512,4,32]{1,3,2,0:T(8,128)(2,1)S(1)} %get-tuple-element.356, s32[]{:T(128)S(6)} %copy.42), kind=kOutput, calls=%fused_computation.8.clone.1 | convolution fusion | flops 276892672 | bytes 794628 | tf_op jit(solution)/shard_map/while/body/eval_jaxpr/hqk,khd->qhd/dot_general | solution.py:58
  170.0 3.1 %fusion.148 = bf16[4,512,32]{1,2,0:T(8,128)(2,1)S(1)} fusion(bf16[1024,4,32]{0,2,1:T(8,128)(2,1)S(1)} %get-tuple-element.358, f32[4,512]{1,0:T(4,128)S(1)} %fusion.147, bf16[1024,4,32]{0,2,1:T(8,128)(2,1)S(1)} %get-tuple-element.357, bf16[8,512,4,32]{1,3,2,0:T(8,128)(2,1)S(1)} %get-tuple-element.356, s32[]{:T(128)S(6)} %copy.42), kind=kOutput, calls=%fused_computation.8.clone.1 | convolution fusion | flops 276892672 | bytes 794628 | tf_op jit(solution)/shard_map/while/body/eval_jaxpr/hqk,khd->qhd/dot_general | solution.py:58
  176.8 3.1 %fusion.148 = bf16[4,512,32]{1,2,0:T(8,128)(2,1)S(1)} fusion(bf16[1024,4,32]{0,2,1:T(8,128)(2,1)S(1)} %get-tuple-element.358, f32[4,512]{1,0:T(4,128)S(1)} %fusion.147, bf16[1024,4,32]{0,2,1:T(8,128)(2,1)S(1)} %get-tuple-element.357, bf16[8,512,4,32]{1,3,2,0:T(8,128)(2,1)S(1)} %get-tuple-element.356, s32[]{:T(128)S(6)} %copy.42), kind=kOutput, calls=%fused_computation.8.clone.1 | convolution fusion | flops 276892672 | bytes 794628 | tf_op jit(solution)/shard_map/while/body/eval_jaxpr/hqk,khd->qhd/dot_general | solution.py:58
  183.6 3.1 %fusion.148 = bf16[4,512,32]{1,2,0:T(8,128)(2,1)S(1)} fusion(bf16[1024,4,32]{0,2,1:T(8,128)(2,1)S(1)} %get-tuple-element.358, f32[4,512]{1,0:T(4,128)S(1)} %fusion.147, bf16[1024,4,32]{0,2,1:T(8,128)(2,1)S(1)} %get-tuple-element.357, bf16[8,512,4,32]{1,3,2,0:T(8,128)(2,1)S(1)} %get-tuple-element.356, s32[]{:T(128)S(6)} %copy.42), kind=kOutput, calls=%fused_computation.8.clone.1 | convolution fusion | flops 276892672 | bytes 794628 | tf_op jit(solution)/shard_map/while/body/eval_jaxpr/hqk,khd->qhd/dot_general | solution.py:58
  190.4 3.1 %fusion.148 = bf16[4,512,32]{1,2,0:T(8,128)(2,1)S(1)} fusion(bf16[1024,4,32]{0,2,1:T(8,128)(2,1)S(1)} %get-tuple-element.358, f32[4,512]{1,0:T(4,128)S(1)} %fusion.147, bf16[1024,4,32]{0,2,1:T(8,128)(2,1)S(1)} %get-tuple-element.357, bf16[8,512,4,32]{1,3,2,0:T(8,128)(2,1)S(1)} %get-tuple-element.356, s32[]{:T(128)S(6)} %copy.42), kind=kOutput, calls=%fused_computation.8.clone.1 | convolution fusion | flops 276892672 | bytes 794628 | tf_op jit(solution)/shard_map/while/body/eval_jaxpr/hqk,khd->qhd/dot_general | solution.py:58
  194.3 4.4 %convolution_convert_fusion.1 = bf16[4,1024,512]{2,1,0:T(8,128)(2,1)} fusion(bf16[4,1024,128]{2,1,0:T(8,128)(2,1)} %bitcast.137, bf16[128,512]{1,0:T(8,128)(2,1)S(1)} %copy-done), kind=kOutput, calls=%fused_computation.52 | convolution fusion | flops 538968064 | bytes 5373952 | tf_op jit(solution)/shard_map/dot_general | solution.py:113
  198.8 8.1 %copy.24 = bf16[4,1024,512]{1,0,2:T(4,128)(2,1)} copy(bf16[4,1024,512]{2,1,0:T(8,128)(2,1)} %convolution_convert_fusion.1) | data formatting | bytes 8388608
  206.9 6.4 %copy.30 = bf16[64,8,4,1024]{3,1,2,0:T(8,128)(2,1)} copy(bf16[64,8,4,1024]{3,2,1,0:T(4,128)(2,1)} %bitcast.132) | data formatting | bytes 8388608
  217.6 5.1 %collective-permute-done = bf16[2,1024,128]{2,1,0:T(8,128)(2,1)S(1)} collective-permute-done((bf16[2,1024,128]{2,1,0:T(8,128)(2,1)S(1)}, bf16[2,1024,128]{2,1,0:T(8,128)(2,1)S(1)}, u32[]{:S(2)}, u32[]{:S(2)}) %collective-permute-start) | collective-permute-done | bytes 524320 | tf_op jit(solution)/shard_map/ppermute | solution.py:15
  222.7 4.4 %collective-permute-done.1 = bf16[2,1024,128]{2,1,0:T(8,128)(2,1)S(1)} collective-permute-done((bf16[2,1024,128]{2,1,0:T(8,128)(2,1)S(1)}, bf16[2,1024,128]{2,1,0:T(8,128)(2,1)S(1)}, u32[]{:S(2)}, u32[]{:S(2)}) %collective-permute-start.1) | collective-permute-done | bytes 524320 | tf_op jit(solution)/shard_map/ppermute | solution.py:18
  229.5 34.2 %reduce-scatter.7.cloned.1.call-done = bf16[128,4096]{1,0:T(8,128)(2,1)} async-done(((bf16[512,4096]{1,0:T(8,128)(2,1)}), bf16[128,4096]{1,0:T(8,128)(2,1)}) %reduce-scatter.7.cloned.1.call-update) | async-done | bytes 1048592
  266.5 29.1 %fusion.88 = bf16[4,1024,128]{2,1,0:T(8,128)(2,1)} fusion(f32[8,1028,128]{2,1,0:T(8,128)} %fusion.85, bf16[4,1024,128]{2,1,0:T(8,128)(2,1)S(1)} %copy.25, bf16[4,1024,128]{2,1,0:T(8,128)(2,1)S(1)} %copy-done.3, f32[128]{0:T(128)S(1)} %get-tuple-element.229, f32[128]{0:T(128)S(1)} %get-tuple-element.230, f32[128]{0:T(128)S(1)} %get-tuple-element.207, ...), kind=kLoop, calls=%fused_computation.62 | loop fusion | flops 28311552 | bytes 55587328 | tf_op jit(solution)/shard_map/convert_element_type | solution.py:131
  (87 shorter events, 59.4 us)
Async XLA Ops:
  6.5 187.8 %copy-start = (bf16[128,512]{1,0:T(8,128)(2,1)S(1)}, bf16[128,512]{1,0:T(8,128)(2,1)}, u32[]{:S(2)}) copy-start(bf16[128,512]{1,0:T(8,128)(2,1)} %param.21) | copy-start | bytes 393220
  6.5 57.8 %all-gather.2.cloned.1.call-start = ((), (), s32[]{:S(2)}) async-start(), calls=%async_computation.2 | async-start | bytes 5242880 | tf_op jit(solution)/shard_map/all_gather | solution.py:68
  7.3 94.0 %reduce-scatter.5.cloned.1.call-start = ((), (), s32[]{:S(2)}) async-start(), calls=%async_computation.3 | async-start | bytes 327680 | tf_op jit(solution)/shard_map/reduce_scatter | solution.py:96
  64.4 3.4 %copy-start.1 = (bf16[4,1024,512]{2,1,0:T(8,128)(2,1)S(1)}, bf16[4,1024,512]{2,1,0:T(8,128)(2,1)}, u32[]{:S(2)}) copy-start(bf16[4,1024,512]{2,1,0:T(8,128)(2,1)} %all-gather.2.cloned.1.call-done) | copy-start | bytes 12582916
  67.8 1.6 copy-start.9
  71.1 1.9 copy-start.2
  73.0 0.7 copy-start.8
  73.7 7.5 %copy-start.4 = (bf16[512,128]{1,0:T(8,128)(2,1)S(1)}, bf16[512,128]{1,0:T(8,128)(2,1)}, u32[]{:S(2)}) copy-start(bf16[512,128]{1,0:T(8,128)(2,1)} %param.18) | copy-start | bytes 393220
  81.1 182.5 %reduce-scatter.7.cloned.1.call-start = ((), (), s32[]{:S(2)}) async-start(), calls=%async_computation.4 | async-start | bytes 5242880
  85.2 25.3 %copy-start.5 = (bf16[512,128]{1,0:T(8,128)(2,1)S(1)}, bf16[512,128]{1,0:T(8,128)(2,1)}, u32[]{:S(2)}) copy-start(bf16[512,128]{1,0:T(8,128)(2,1)} %param.20) | copy-start | bytes 393220
  85.2 25.6 %copy-start.6 = (bf16[512,128]{1,0:T(8,128)(2,1)S(1)}, bf16[512,128]{1,0:T(8,128)(2,1)}, u32[]{:S(2)}) copy-start(bf16[512,128]{1,0:T(8,128)(2,1)} %param.19) | copy-start | bytes 393220
  213.4 4.2 %copy-start.7 = (f32[25,128]{1,0:T(8,128)S(1)}, f32[25,128]{1,0:T(8,128)}, u32[]{:S(2)}) copy-start(f32[25,128]{1,0:T(8,128)} %param.22) | copy-start | bytes 38404
  214.7 8.0 %collective-permute-start = (bf16[2,1024,128]{2,1,0:T(8,128)(2,1)S(1)}, bf16[2,1024,128]{2,1,0:T(8,128)(2,1)S(1)}, u32[]{:S(2)}, u32[]{:S(2)}) collective-permute-start(bf16[2,1024,128]{2,1,0:T(8,128)(2,1)S(1)} %get-tuple-element.204), channel_id=1, source_target_pairs={{0,8},{8,16},{16,24},{1,9},{9,17},{17,25},{2,10},{10,18},{18,26},{... | collective-permute-start | bytes 1572872 | tf_op jit(solution)/shard_map/ppermute | solution.py:15
  216.0 11.1 %collective-permute-start.1 = (bf16[2,1024,128]{2,1,0:T(8,128)(2,1)S(1)}, bf16[2,1024,128]{2,1,0:T(8,128)(2,1)S(1)}, u32[]{:S(2)}, u32[]{:S(2)}) collective-permute-start(bf16[2,1024,128]{2,1,0:T(8,128)(2,1)S(1)} %get-tuple-element.205), channel_id=1, source_target_pairs={{8,0},{16,8},{24,16},{9,1},{17,9},{25,17},{10,2},{18,10},{26,18},{... | collective-permute-start | bytes 1572872 | tf_op jit(solution)/shard_map/ppermute | solution.py:18
  229.5 37.0 %copy-start.3 = (bf16[4,1024,128]{2,1,0:T(8,128)(2,1)S(1)}, bf16[4,1024,128]{2,1,0:T(8,128)(2,1)}, u32[]{:S(2)}) copy-start(bf16[4,1024,128]{2,1,0:T(8,128)(2,1)} %param.14) | copy-start | bytes 3145732
Sparse Core Ops, SparseCore 0:
  9.2 55.1 all-gather.1
  81.2 19.9 reduce-scatter.4
  213.5 50.1 reduce-scatter.6
where the time goes:
time: 303 us; the launch traced here: 302 us
  waiting for transfers between devices  113 us (37%)
  matrix products  63.1 us (21%)
  other arithmetic  42 us (14%)
  blocking collectives  37.5 us (12%)
  local copies, waits for them, and re-layouts  29.8 us (10%)
  between operations  13.4 us (4%)
    all_gather x1, waiting for transfers between devices, shards(): whole = lax.all_gather(tokens, 'head', axis=2, tiled=True)  53.4 us
    unnamed x4, waiting for transfers between devices  34.9 us
    convert_element_type x1, other arithmetic, shards(): return total.astype(jnp.bfloat16)  29.1 us
    dot_general x8, matrix products, one_block(): jnp.einsum('hqk,khd->qhd', probs, value_heads, preferred_element_type=jnp...  24.7 us
    sub x8, matrix products, one_block(): expo = jnp.exp(scores - top)  23.4 us
    unnamed x25, local copies, waits for them, and re-layouts  20.7 us
    reduce_scatter x1, waiting for transfers between devices, shards(): lax.psum_scatter(sample_points(normed_here, col_table, row_table, share_r...  15.3 us
    all_gather x1, blocking collectives, shards(): lax.all_gather(key_share, 'band', axis=0, tiled=True)  14.3 us
  transfers between devices with their start and end apart: 5, of which 5 were waited for; matrix products, arithmetic and copies ran while one was open for 4% of the time, Pallas kernels for 0%

commit v1 on v0

--- a/solution.py
+++ b/solution.py
@@ -65,7 +65,12 @@
     tokens, corner_row, corner_col, fraction, w_query, w_key, w_value, w_out, conv_kernel, norm_gain
 ):
     band_rows, columns, channels = tokens.shape
-    whole = lax.all_gather(tokens, "head", axis=2, tiled=True)
+    ring = [tokens]
+    for hop in range(3):
+        ring.append(lax.ppermute(ring[-1], "head", [(dev, (dev + 1) % 4) for dev in range(4)]))
+    whole = jnp.roll(
+        jnp.concatenate(ring[::-1], axis=2), (lax.axis_index("head") + 1) * ring[0].shape[2], axis=2
+    )
     normed = layer_norm(whole, norm_gain)
     width = normed.shape[2]
     count = band_rows * columns

time: 303 us -> 324 us (1.069)
  waiting for transfers between devices: 113 us -> 125 us
  starting transfers between devices: 2.92 us -> 9.89 us
  local copies, waits for them, and re-layouts: 29.8 us -> 34.3 us
    ppermute x0 -> x3, waiting for transfers between devices: none -> 69.5 us  [shards(): lax.ppermute(ring[-1], 'head', [(dev, (dev + 1) % 4) for dev in range(4)])]
    all_gather x1 -> x0, waiting for transfers between devices: 53.4 us -> none  [shards(): whole = lax.all_gather(tokens, 'head', axis=2, tiled=True)]
    unnamed x25 -> x40, local copies, waits for them, and re-layouts: 20.7 us -> 24.8 us
    ppermute x0 -> x3, starting transfers between devices: none -> 3.76 us  [shards(): lax.ppermute(ring[-1], 'head', [(dev, (dev + 1) % 4) for dev in range(4)])]
    ppermute x1, waiting for transfers between devices: 5.08 us -> 1.46 us  [padded_2(): lax.ppermute(lax.slice_in_dim(block, block.shape[dim] - width, None, axis...]
    ppermute x1, starting transfers between devices: 1.32 us -> 4.8 us  [padded_2(): lax.ppermute(lax.slice_in_dim(block, block.shape[dim] - width, None, axis...]
    unnamed x4 -> x3, waiting for transfers between devices: 34.9 us -> 34 us
  transfers between devices with their start and end apart: 5 -> 7, of which waited for: 5 -> 7; matrix products, arithmetic and copies ran while one was open for 4% -> 4% of each run, Pallas kernels for 0% -> 0%
where the time goes in v1:
time: 324 us; the launch traced here: 323 us
  waiting for transfers between devices  125 us (39%)
  matrix products  63.1 us (19%)
  other arithmetic  39.6 us (12%)
  blocking collectives  37.5 us (12%)
  local copies, waits for them, and re-layouts  34.3 us (11%)
  between operations  13.7 us (4%)
  starting transfers between devices  9.89 us (3%)
    ppermute x3, waiting for transfers between devices, shards(): lax.ppermute(ring[-1], 'head', [(dev, (dev + 1) % 4) for dev in range(4)])  69.5 us
    unnamed x3, waiting for transfers between devices  34 us
    convert_element_type x1, other arithmetic, shards(): return total.astype(jnp.bfloat16)  28.7 us
    unnamed x40, local copies, waits for them, and re-layouts  24.8 us
    dot_general x8, matrix products, one_block(): jnp.einsum('hqk,khd->qhd', probs, value_heads, preferred_element_type=jnp...  24.8 us
    sub x8, matrix products, one_block(): expo = jnp.exp(scores - top)  23.5 us
    reduce_scatter x1, waiting for transfers between devices, shards(): lax.psum_scatter(sample_points(normed_here, col_table, row_table, share_r...  15.1 us
    all_gather x1, blocking collectives, shards(): lax.all_gather(key_share, 'band', axis=0, tiled=True)  14.2 us
  transfers between devices with their start and end apart: 7, of which 7 were waited for; matrix products, arithmetic and copies ran while one was open for 4% of the time, Pallas kernels for 0%

profile of v1, /device:TPU:0, one launch (start us, length us, event | category | flops | bytes accessed | tf_op | source)
XLA Modules:
  0.0 323.2 jit_solution(7547039699296865175)
XLA Ops:
  9.5 24.3 %collective-permute-done = bf16[4,1024,128]{2,1,0:T(8,128)(2,1)S(1)} collective-permute-done((bf16[4,1024,128]{2,1,0:T(8,128)(2,1)}, bf16[4,1024,128]{2,1,0:T(8,128)(2,1)S(1)}, u32[]{:S(2)}, u32[]{:S(2)}) %collective-permute-start) | collective-permute-done | bytes 1048608 | tf_op jit(solution)/shard_map/ppermute | solution.py:70
  34.6 24.4 %collective-permute-done.1 = bf16[4,1024,128]{2,1,0:T(8,128)(2,1)S(1)} collective-permute-done((bf16[4,1024,128]{2,1,0:T(8,128)(2,1)S(1)}, bf16[4,1024,128]{2,1,0:T(8,128)(2,1)S(1)}, u32[]{:S(2)}, u32[]{:S(2)}) %collective-permute-start.1) | collective-permute-done | bytes 1048608 | tf_op jit(solution)/shard_map/ppermute | solution.py:70
  62.7 20.7 %collective-permute-done.2 = bf16[4,1024,128]{2,1,0:T(8,128)(2,1)S(1)} collective-permute-done((bf16[4,1024,128]{2,1,0:T(8,128)(2,1)S(1)}, bf16[4,1024,128]{2,1,0:T(8,128)(2,1)S(1)}, u32[]{:S(2)}, u32[]{:S(2)}) %collective-permute-start.2) | collective-permute-done | bytes 1048608 | tf_op jit(solution)/shard_map/ppermute | solution.py:70
  94.9 6.7 %while.25 = (s32[]{:T(128)}, f32[1024,128]{0,1:T(8,128)S(1)}, f32[1024,4]{0,1:T(4,128)S(1)}, bf16[4,1024,128]{2,1,0:T(8,128)(2,1)S(1)}, s32[1024]{0:T(1024)S(1)}...) while((s32[]{:T(128)}, f32[1024,128]{0,1:T(8,128)S(1)}, ...), condition=%wide.region_3.4_spmd.clone, body=%wide.region_2.3_spmd.clone.sunk | while | flops 277217280 | bytes 1335423 | solution.py:39
  102.7 3.4 %convolution_convert_fusion = bf16[4096,128]{1,0:T(8,128)(2,1)S(1)} fusion(bf16[4096,512]{1,0:T(8,128)(2,1)} %bitcast.130, bf16[512,128]{1,0:T(8,128)(2,1)S(1)} %copy-done.8), kind=kOutput, calls=%fused_computation.50 | convolution fusion | flops 537395200 | bytes 5373952 | tf_op jit(solution)/shard_map/dot_general | solution.py:77
  107.4 15.1 %reduce-scatter.5.cloned.1.call-done = bf16[256,128]{0,1:T(8,128)(2,1)} async-done(((bf16[1024,128]{0,1:T(8,128)(2,1)}), bf16[256,128]{0,1:T(8,128)(2,1)}) %reduce-scatter.5.cloned.1.call-update) | async-done | bytes 65552 | tf_op jit(solution)/shard_map/reduce_scatter | solution.py:101
  122.5 9.2 %all_gather.9 = bf16[256,512]{0,1:T(8,128)(2,1)S(1)} all-gather(bf16[256,128]{0,1:T(8,128)(2,1)} %reduce-scatter.5.cloned.1.call-done), channel_id=1, replica_groups=mesh['band'=4,'head'=4,'dp'=2] {'head'}, dimensions={1}, use_global_device_ids=true | all-gather | bytes 327680 | tf_op jit(solution)/shard_map/all_gather | solution.py:109
  132.0 14.2 %all_gather.10 = bf16[1024,128]{1,0:T(8,128)(2,1)S(1)} all-gather(bf16[256,128]{1,0:T(8,128)(2,1)S(1)} %convolution_convert_fusion.3), channel_id=1, replica_groups=mesh['band'=4,'head'=4,'dp'=2] {'band'}, dimensions={0}, use_global_device_ids=true | all-gather | bytes 327680 | tf_op jit(solution)/shard_map/all_gather | solution.py:113
  146.7 14.0 %all_gather.11 = bf16[1024,128]{1,0:T(8,128)(2,1)S(1)} all-gather(bf16[256,128]{1,0:T(8,128)(2,1)S(1)} %convolution_convert_fusion.2), channel_id=1, replica_groups=mesh['band'=4,'head'=4,'dp'=2] {'band'}, dimensions={0}, use_global_device_ids=true | all-gather | bytes 327680 | tf_op jit(solution)/shard_map/all_gather | solution.py:114
  160.9 54.7 %while.24 = (s32[]{:T(128)}, bf16[8,512,128]{2,1,0:T(8,128)(2,1)}, bf16[8,512,4,32]{1,3,2,0:T(8,128)(2,1)S(1)}, bf16[1024,4,32]{0,2,1:T(8,128)(2,1)S(1)}, bf16[1024,4,32]{0,2,1:T(8,128)(2,1)S(1)}, /*index=5*/s32[]{:T(128)}) while((s32[]{:T(128)}, bf16[8,512,128]{2,1,0:T(8,128)(2,1)}, bf16[8,512,4,32]{1,3,2,0:T(8,128)(2,1)S(1)}, ...), condition=%wide.region_8.9_spmd, body=%wide.region_5.8_spmd.sunk | while | flops 417402880 | bytes 1720409 | solution.py:61
  163.8 3.1 fusion.148
  170.6 3.1 fusion.148
  184.3 3.1 fusion.148
  191.2 3.1 fusion.148
  198.0 3.1 fusion.148
  204.8 3.1 fusion.148
  211.7 3.1 fusion.148
  215.6 4.4 %convolution_convert_fusion.1 = bf16[4,1024,512]{2,1,0:T(8,128)(2,1)} fusion(bf16[4,1024,128]{2,1,0:T(8,128)(2,1)} %bitcast.137, bf16[128,512]{1,0:T(8,128)(2,1)S(1)} %copy-done), kind=kOutput, calls=%fused_computation.52 | convolution fusion | flops 538968064 | bytes 5373952 | tf_op jit(solution)/shard_map/dot_general | solution.py:118
  220.0 8.1 %copy.24 = bf16[4,1024,512]{1,0,2:T(4,128)(2,1)} copy(bf16[4,1024,512]{2,1,0:T(8,128)(2,1)} %convolution_convert_fusion.1) | data formatting | bytes 8388608
  228.1 6.4 %copy.30 = bf16[64,8,4,1024]{3,1,2,0:T(8,128)(2,1)} copy(bf16[64,8,4,1024]{3,2,1,0:T(4,128)(2,1)} %bitcast.132) | data formatting | bytes 8388608
  237.3 4.8 %collective-permute-start.3 = (bf16[2,1024,128]{2,1,0:T(8,128)(2,1)S(1)}, bf16[2,1024,128]{2,1,0:T(8,128)(2,1)S(1)}, u32[]{:S(2)}, u32[]{:S(2)}) collective-permute-start(bf16[2,1024,128]{2,1,0:T(8,128)(2,1)S(1)} %get-tuple-element.204), channel_id=1, source_target_pairs={{0,8},{8,16},{16,24},{1,9},{9,17},{17,25},{2,10},{10,18},{18,26},{... | collective-permute-start | bytes 1572872 | tf_op jit(solution)/shard_map/ppermute | solution.py:15
  242.1 4.9 %collective-permute-done.4 = bf16[2,1024,128]{2,1,0:T(8,128)(2,1)S(1)} collective-permute-done((bf16[2,1024,128]{2,1,0:T(8,128)(2,1)S(1)}, bf16[2,1024,128]{2,1,0:T(8,128)(2,1)S(1)}, u32[]{:S(2)}, u32[]{:S(2)}) %collective-permute-start.4) | collective-permute-done | bytes 524320 | tf_op jit(solution)/shard_map/ppermute | solution.py:18
  250.9 33.9 %reduce-scatter.7.cloned.1.call-done = bf16[128,4096]{1,0:T(8,128)(2,1)} async-done(((bf16[512,4096]{1,0:T(8,128)(2,1)}), bf16[128,4096]{1,0:T(8,128)(2,1)}) %reduce-scatter.7.cloned.1.call-update) | async-done | bytes 1048592
  287.7 28.7 %fusion.88 = bf16[4,1024,128]{2,1,0:T(8,128)(2,1)} fusion(f32[8,1028,128]{2,1,0:T(8,128)} %fusion.85, bf16[4,1024,128]{2,1,0:T(8,128)(2,1)S(1)} %copy.25, bf16[4,1024,128]{2,1,0:T(8,128)(2,1)S(1)} %copy-done.2, f32[128]{0:T(128)S(1)} %get-tuple-element.229, f32[128]{0:T(128)S(1)} %get-tuple-element.230, f32[128]{0:T(128)S(1)} %get-tuple-element.207, ...), kind=kLoop, calls=%fused_computation.62 | loop fusion | flops 28311552 | bytes 55587328 | tf_op jit(solution)/shard_map/convert_element_type | solution.py:136
  (106 shorter events, 70.8 us)
Async XLA Ops:
  6.5 209.0 %copy-start = (bf16[128,512]{1,0:T(8,128)(2,1)S(1)}, bf16[128,512]{1,0:T(8,128)(2,1)}, u32[]{:S(2)}) copy-start(bf16[128,512]{1,0:T(8,128)(2,1)} %param.21) | copy-start | bytes 393220
  6.5 116.0 %reduce-scatter.5.cloned.1.call-start = ((), (), s32[]{:S(2)}) async-start(), calls=%async_computation.2 | async-start | bytes 327680 | tf_op jit(solution)/shard_map/reduce_scatter | solution.py:101
  6.5 27.3 %collective-permute-start = (bf16[4,1024,128]{2,1,0:T(8,128)(2,1)}, bf16[4,1024,128]{2,1,0:T(8,128)(2,1)S(1)}, u32[]{:S(2)}, u32[]{:S(2)}) collective-permute-start(bf16[4,1024,128]{2,1,0:T(8,128)(2,1)} %param.14), channel_id=1, source_target_pairs={{0,2},{2,4},{4,6},{6,0},{1,3},{3,5},{5,7},{7,1},{8,10},{10,12},{12... | collective-permute-start | bytes 3145736 | tf_op jit(solution)/shard_map/ppermute | solution.py:70
  33.8 25.2 %collective-permute-start.1 = (bf16[4,1024,128]{2,1,0:T(8,128)(2,1)S(1)}, bf16[4,1024,128]{2,1,0:T(8,128)(2,1)S(1)}, u32[]{:S(2)}, u32[]{:S(2)}) collective-permute-start(bf16[4,1024,128]{2,1,0:T(8,128)(2,1)S(1)} %collective-permute-done), channel_id=1, source_target_pairs={{0,2},{2,4},{4,6},{6,0},{1,3},{3,5},{5,7},{7,1},{8,10},{10,12},{12... | collective-permute-start | bytes 3145736 | tf_op jit(solution)/shard_map/ppermute | solution.py:70
  59.1 24.4 %collective-permute-start.2 = (bf16[4,1024,128]{2,1,0:T(8,128)(2,1)S(1)}, bf16[4,1024,128]{2,1,0:T(8,128)(2,1)S(1)}, u32[]{:S(2)}, u32[]{:S(2)}) collective-permute-start(bf16[4,1024,128]{2,1,0:T(8,128)(2,1)S(1)} %collective-permute-done.1), channel_id=1, source_target_pairs={{0,2},{2,4},{4,6},{6,0},{1,3},{3,5},{5,7},{7,1},{8,10},{10,12},{12... | collective-permute-start | bytes 3145736 | tf_op jit(solution)/shard_map/ppermute | solution.py:70
  83.4 1.0 copy-start.3
  84.7 1.2 copy-start.2
  85.1 1.3 copy-start.4
  88.5 1.8 copy-start.13
  91.9 1.9 copy-start.1
  93.9 1.0 copy-start.7
  93.9 1.0 copy-start.12
  94.9 7.7 %copy-start.8 = (bf16[512,128]{1,0:T(8,128)(2,1)S(1)}, bf16[512,128]{1,0:T(8,128)(2,1)}, u32[]{:S(2)}) copy-start(bf16[512,128]{1,0:T(8,128)(2,1)} %param.18) | copy-start | bytes 393220
  101.6 1.1 copy-start.5
  102.4 182.4 %reduce-scatter.7.cloned.1.call-start = ((), (), s32[]{:S(2)}) async-start(), calls=%async_computation.3 | async-start | bytes 5242880
  106.6 25.1 %copy-start.9 = (bf16[512,128]{1,0:T(8,128)(2,1)S(1)}, bf16[512,128]{1,0:T(8,128)(2,1)}, u32[]{:S(2)}) copy-start(bf16[512,128]{1,0:T(8,128)(2,1)} %param.19) | copy-start | bytes 393220
  107.1 39.3 %copy-start.10 = (bf16[512,128]{1,0:T(8,128)(2,1)S(1)}, bf16[512,128]{1,0:T(8,128)(2,1)}, u32[]{:S(2)}) copy-start(bf16[512,128]{1,0:T(8,128)(2,1)} %param.20) | copy-start | bytes 393220
  234.5 7.5 %copy-start.11 = (f32[25,128]{1,0:T(8,128)S(1)}, f32[25,128]{1,0:T(8,128)}, u32[]{:S(2)}) copy-start(f32[25,128]{1,0:T(8,128)} %param.22) | copy-start | bytes 38404
  234.6 13.9 %copy-start.6 = (bf16[4,1024,128]{2,1,0:T(8,128)(2,1)S(1)}, bf16[4,1024,128]{2,1,0:T(8,128)(2,1)}, u32[]{:S(2)}) copy-start(bf16[4,1024,128]{2,1,0:T(8,128)(2,1)} %copy-done.5) | copy-start | bytes 3145732
  236.0 11.1 %collective-permute-start.4 = (bf16[2,1024,128]{2,1,0:T(8,128)(2,1)S(1)}, bf16[2,1024,128]{2,1,0:T(8,128)(2,1)S(1)}, u32[]{:S(2)}, u32[]{:S(2)}) collective-permute-start(bf16[2,1024,128]{2,1,0:T(8,128)(2,1)S(1)} %get-tuple-element.205), channel_id=1, source_target_pairs={{8,0},{16,8},{24,16},{9,1},{17,9},{25,17},{10,2},{18,10},{26,18},{... | collective-permute-start | bytes 1572872 | tf_op jit(solution)/shard_map/ppermute | solution.py:18
  237.3 11.2 %collective-permute-start.3 = (bf16[2,1024,128]{2,1,0:T(8,128)(2,1)S(1)}, bf16[2,1024,128]{2,1,0:T(8,128)(2,1)S(1)}, u32[]{:S(2)}, u32[]{:S(2)}) collective-permute-start(bf16[2,1024,128]{2,1,0:T(8,128)(2,1)S(1)} %get-tuple-element.204), channel_id=1, source_target_pairs={{0,8},{8,16},{16,24},{1,9},{9,17},{17,25},{2,10},{10,18},{18,26},{... | collective-permute-start | bytes 1572872 | tf_op jit(solution)/shard_map/ppermute | solution.py:15
Sparse Core Ops, SparseCore 0:
  102.6 19.9 reduce-scatter.4
  234.7 50.1 reduce-scatter.6
